TPU v7x, 256 devices: a whole 4x4x8 slice. The times are simulated.
256 devices in a mesh: gx: 32 (over x, z_hi, y), vz: 8 (over z_lo, core).
Axes of the slice: x: 4, y: 4, z: 8 (z_hi: 2, z_lo: 4; z = z_hi * 4 + z_lo), core: 2. Of those that a mesh axis runs over, the one named last changes fastest.
Arguments:
- density: float32 [24, 256, 64, 256], P('vz', 'gx'), may hold values from 0.02 to 2.5, as said below
- shift_depth: int32 [16], replicated, may hold values from -20 to 20, as said below
- sub_cell: float32 [16], replicated, may hold values from 0 to 1
- gravity_kick: float32 [256, 64], P('gx'), may hold values from -0.9 to 0.9
- collision: float32 [256, 64], P('gx'), may hold values from 0.1 to 10
Outputs:
- relaxed: float32 [24, 256, 64, 256], P('vz', 'gx')
Inputs may be any that keep to these rules, and one draw needn't show every extreme that they name: `density`: every value is positive. `shift_depth`: some x velocity has 20 and some has -20.
All inputs are finite; a program needn't handle non-finite values.
Results may differ from a plain program's by a relative error of at most 0.00002.
Values sent between devices are 32-bit elements; how exact they have to be, the bound alone decides.
A program may use at most 64 MiB of HBM per device.

v0:
```python
import jax
import jax.numpy as jnp
from jax import lax
from jax.sharding import Mesh
from jax.sharding import PartitionSpec as P

NVX = 16
NVY = 16
VZ = ("vz_0", "vz_1")


def grouped_exchange(x, axis, split_dim, concat_dim, work, item_dim, out_dim):

    def moved(group):
        return lax.all_to_all(group, axis, split_axis=split_dim, concat_axis=concat_dim, tiled=True)

    items = jax.tree.leaves(x)[0].shape[item_dim]
    ends = [items * k // 2 for k in range(2 + 1)] if items % 2 == 0 else [0, items]
    groups = [
        jax.tree.map(lambda a: lax.slice_in_dim(a, low, high, axis=item_dim), x)
        for low, high in zip(ends, ends[1:])
    ]
    arrived = [moved(group) for group in groups]
    made = [work(group) for group in arrived]
    return jax.tree.map(lambda *parts: jnp.concatenate(parts, axis=out_dim), *made)


def padded_2(cells, sides, width):
    for axis, dim in sides:
        count = lax.axis_size(axis)
        ends = count - 1
        head = lax.slice_in_dim(cells, 0, width, axis=dim)
        tail = lax.slice_in_dim(cells, cells.shape[dim] - width, cells.shape[dim], axis=dim)
        cells = jnp.concatenate(
            [
                lax.ppermute(tail, axis, [(i, (i + 1) % count) for i in range(ends)]),
                cells,
                lax.ppermute(head, axis, [((i + 1) % count, i) for i in range(ends)]),
            ],
            axis=dim,
        )
    return cells


def one_axis_at_a_time(x, axes):
    for axis in axes:
        x = lax.psum(x, axis)
    return x


def velocity_values(indices, count, extent):
    return (indices.astype(jnp.float32) - (count - 1) / 2.0) * (extent / count)


def shift_groups(source, starts_near, starts_far, length, sub_cell, axis_x):
    lead = source.shape[:-1]
    grouped = source.reshape(lead + (NVX, NVY))
    pieces = []
    for group in range(NVX):
        column_set = lax.index_in_dim(grouped, group, axis=len(lead), keepdims=False)
        near = lax.dynamic_slice_in_dim(column_set, starts_near[group], length, axis_x)
        far = lax.dynamic_slice_in_dim(column_set, starts_far[group], length, axis_x)
        pieces.append((1.0 - sub_cell[group]) * near + sub_cell[group] * far)
    joined = jnp.stack(pieces, axis=len(lead))
    out_lead = joined.shape[: len(lead)]
    return joined.reshape(out_lead + (NVX * NVY,))


def per_device(density, shift_depth, sub_cell, gravity_kick, collision):
    slab_planes, strip_cols, rows_y, pairs = density.shape
    slab_count = lax.axis_size(VZ)
    total_vz = slab_planes * slab_count
    speed_x = jnp.repeat(velocity_values(jnp.arange(NVX, dtype=jnp.int32), NVX, 9.0), NVY)
    speed_y = jnp.tile(velocity_values(jnp.arange(NVY, dtype=jnp.int32), NVY, 9.0), NVX)
    plane_ids = lax.axis_index(VZ) * slab_planes + jnp.arange(slab_planes, dtype=jnp.int32)
    speed_z = velocity_values(plane_ids, total_vz, 9.6)
    measure_element = 9.0 / NVX * (9.0 / NVY) * (9.6 / total_vz)

    def advect_columns(block):
        width_x = block.shape[1]
        doubled = jnp.concatenate([block, block], axis=1)
        starts_near = jnp.mod(width_x - shift_depth, width_x)
        starts_far = jnp.mod(width_x - shift_depth - 1, width_x)
        shifted = shift_groups(doubled, starts_near, starts_far, width_x, sub_cell, 1)
        return lax.all_to_all(shifted, "gx", split_axis=1, concat_axis=2, tiled=True)

    moved = grouped_exchange(density, "gx", 2, 1, advect_columns, 0, 0)
    padded = padded_2(moved, ((VZ, 0),), 1)
    kick = gravity_kick[None, :, :, None]
    weight_accelerated = (
        (1.0 - jnp.abs(kick)) * moved
        + jnp.maximum(kick, 0.0) * padded[:-2]
        + jnp.maximum(-kick, 0.0) * padded[2:]
    )
    plane_sums = jnp.sum(weight_accelerated, axis=3)
    local_mass = jnp.sum(plane_sums, axis=0)
    local_flow_x = jnp.sum(weight_accelerated * speed_x, axis=(0, 3))
    local_flow_y = jnp.sum(weight_accelerated * speed_y, axis=(0, 3))
    local_flow_z = jnp.sum(plane_sums * speed_z[:, None, None], axis=0)
    energy_terms = speed_x**2 + speed_y**2
    local_energy = jnp.sum(weight_accelerated * energy_terms, axis=(0, 3)) + jnp.sum(
        plane_sums * (speed_z**2)[:, None, None], axis=0
    )
    mass_sum, momentum_x, momentum_y, momentum_z, energy_sum = (
        one_axis_at_a_time(local_mass, VZ),
        one_axis_at_a_time(local_flow_x, VZ),
        one_axis_at_a_time(local_flow_y, VZ),
        one_axis_at_a_time(local_flow_z, VZ),
        one_axis_at_a_time(local_energy, VZ),
    )
    matter_per_cell = measure_element * mass_sum
    flow_x = measure_element * momentum_x / matter_per_cell
    flow_y = measure_element * momentum_y / matter_per_cell
    flow_z = measure_element * momentum_z / matter_per_cell
    speed_sq = flow_x**2 + flow_y**2 + flow_z**2
    motion_warmth = (measure_element * energy_sum - matter_per_cell * speed_sq) / (
        3.0 * matter_per_cell
    )
    deviation_square = (
        (speed_x - flow_x[None, :, :, None]) ** 2
        + (speed_y - flow_y[None, :, :, None]) ** 2
        + (speed_z[:, None, None, None] - flow_z[None, :, :, None]) ** 2
    )
    agitation_width = matter_per_cell * (2.0 * jnp.pi * motion_warmth) ** (-1.5)
    equilibrium_profile = agitation_width[None, :, :, None] * jnp.exp(
        -deviation_square / (2.0 * motion_warmth[None, :, :, None])
    )
    rate = collision[None, :, :, None]
    return (weight_accelerated + rate * equilibrium_profile) / (1.0 + rate)


def solution(mesh):
    torus = Mesh(mesh.devices.reshape(mesh.shape["gx"], 4, 2), ("gx", "vz_0", "vz_1"))
    return jax.shard_map(
        per_device,
        mesh=torus,
        in_specs=(P(VZ, "gx", None, None), P(), P(), P("gx", None), P("gx", None)),
        out_specs=P(VZ, "gx", None, None),
        check_vma=False,
    )
```

profile of v0, /device:TPU:1, one launch (start us, length us, event | category | flops | bytes accessed | tf_op | source)
XLA Modules:
  0.0 214.6 jit_solution(9858659908536691685)
XLA Ops:
  0.0 3.5 %copy.57 = f32[3,8,64,256]{3,1,0,2:T(8,128)} copy(f32[3,8,64,256]{3,2,1,0:T(8,128)} %param.5) | data formatting | bytes 3145728 | tf_op args[0]
  3.5 14.6 %all-to-all-start = ((f32[3,8,64,256]{3,1,0,2:T(8,128)}), f32[3,8,64,256]{3,1,0,2:T(8,128)S(1)}, u32[]{:S(2)}, u32[]{:S(2)}) async-start(f32[3,8,64,256]{3,1,0,2:T(8,128)} %copy.57), calls=%async_computation | async-start | bytes 3145728 | tf_op jit(solution)/shard_map/all_to_all | solution.py:15
  18.1 0.7 fusion.29
  20.1 0.7 fusion.28
  59.7 0.7 fusion.27
  90.3 0.1 copy.85
  90.4 6.6 %concatenate.13 = f32[3,256,2,16,16]{4,3,1,2,0:T(8,128)} reshape(f32[3,32,8,2,256]{4,2,1,3,0:T(8,128)S(1)} %bitcast.69) | data formatting | bytes 3145728 | tf_op jit(solution)/shard_map/concatenate | solution.py:81
  97.1 8.9 %copy.59 = f32[3,256,2,16,16]{1,4,3,2,0:T(8,128)S(1)} copy(f32[3,256,2,16,16]{4,3,1,2,0:T(8,128)} %concatenate.13) | data formatting | bytes 3145728 | tf_op jit(solution)/shard_map/concatenate | solution.py:81
  106.0 0.1 fusion.18
  106.1 0.1 fusion.4
  106.2 0.7 add_dynamic-update-slice_fusion.14
  107.0 0.8 add_dynamic-update-slice_fusion.13
  107.7 0.7 add_dynamic-update-slice_fusion.12
  108.5 0.7 add_dynamic-update-slice_fusion.11
  109.2 0.8 add_dynamic-update-slice_fusion.10
  109.9 0.7 add_dynamic-update-slice_fusion.9
  110.6 0.8 add_dynamic-update-slice_fusion.8
  111.3 0.8 add_dynamic-update-slice_fusion.7
  112.1 0.7 add_dynamic-update-slice_fusion.6
  112.8 0.7 add_dynamic-update-slice_fusion.5
  113.6 0.7 add_dynamic-update-slice_fusion.4
  114.3 0.8 add_dynamic-update-slice_fusion.3
  115.1 0.7 add_dynamic-update-slice_fusion.2
  115.9 0.8 add_dynamic-update-slice_fusion.1
  116.7 0.7 add_dynamic-update-slice_fusion
  117.4 0.8 fusion.21
  118.2 2.1 copy.61
  120.3 11.8 %all-to-all-start.1 = ((f32[3,256,2,256]{3,2,0,1:T(2,128)}), f32[3,256,2,256]{3,2,0,1:T(2,128)S(1)}, u32[]{:S(2)}, u32[]{:S(2)}) async-start(f32[3,256,2,256]{3,2,0,1:T(2,128)} %copy.61), calls=%async_computation.1 | async-start | bytes 3145728 | tf_op jit(solution)/shard_map/all_to_all | solution.py:85
  132.3 0.1 copy.66
  132.6 0.1 copy.68
  132.7 27.6 %all-to-all-done.1 = f32[3,256,2,256]{3,2,0,1:T(2,128)S(1)} async-done(((f32[3,256,2,256]{3,2,0,1:T(2,128)}), f32[3,256,2,256]{3,2,0,1:T(2,128)S(1)}, u32[]{:S(2)}, u32[]{:S(2)}) %all-to-all-start.1) | async-done | bytes 1572896 | tf_op jit(solution)/shard_map/all_to_all | solution.py:85
  160.2 0.1 copy.84
  160.5 16.7 %collective-permute-start.1 = (f32[1,8,64,256]{3,1,2,0:T(8,128)S(1)}, f32[1,8,64,256]{3,1,2,0:T(8,128)S(1)}, u32[]{:S(2)}, u32[]{:S(2)}) collective-permute-start(f32[1,8,64,256]{3,1,2,0:T(8,128)S(1)} %bitcast.71), channel_id=1, source_target_pairs={{1,0},{2,1},{3,2},{4,3},{5,4},{6,5},{7,6},{9,8},{10,9},{11,10},{12... | collective-permute-start | bytes 1572872 | tf_op jit(solution)/shard_map/ppermute | solution.py:38
  177.2 0.9 copy.65
  178.1 3.2 %collective-permute-start = (f32[1,8,64,256]{3,1,2,0:T(8,128)}, f32[1,8,64,256]{3,1,2,0:T(8,128)S(1)}, u32[]{:S(2)}, u32[]{:S(2)}) collective-permute-start(f32[1,8,64,256]{3,1,2,0:T(8,128)} %bitcast.55), channel_id=1, source_target_pairs={{0,1},{1,2},{2,3},{3,4},{4,5},{5,6},{6,7},{8,9},{9,10},{10,11},{11... | collective-permute-start | bytes 1572872 | tf_op jit(solution)/shard_map/ppermute | solution.py:36
  181.3 0.1 copy.80
  181.4 0.2 copy.63
  181.6 3.8 %collective-permute-done.1 = f32[1,8,64,256]{3,1,2,0:T(8,128)S(1)} collective-permute-done((f32[1,8,64,256]{3,1,2,0:T(8,128)S(1)}, f32[1,8,64,256]{3,1,2,0:T(8,128)S(1)}, u32[]{:S(2)}, u32[]{:S(2)}) %collective-permute-start.1) | collective-permute-done | bytes 524320 | tf_op jit(solution)/shard_map/ppermute | solution.py:38
  185.4 2.3 %collective-permute-done = f32[1,8,64,256]{3,1,2,0:T(8,128)S(1)} collective-permute-done((f32[1,8,64,256]{3,1,2,0:T(8,128)}, f32[1,8,64,256]{3,1,2,0:T(8,128)S(1)}, u32[]{:S(2)}, u32[]{:S(2)}) %collective-permute-start) | collective-permute-done | bytes 524320 | tf_op jit(solution)/shard_map/ppermute | solution.py:36
  187.7 1.4 multiply_reduce_fusion
  189.2 0.1 multiply_reduce_fusion.3
  189.6 12.9 %all-reduce = (f32[8,64]{1,0:T(8,128)S(1)}, f32[8,64]{1,0:T(8,128)S(1)}, f32[8,64]{1,0:T(8,128)S(1)}, f32[8,64]{1,0:T(8,128)S(1)}, f32[8,64]{1,0:T(8,128)S(1)}) all-reduce(f32[8,64]{1,0:T(8,128)S(1)} %copy.69, f32[8,64]{1,0:T(8,128)S(1)} %add.335, f32[8,64]{1,0:T(8,128)S(1)} %copy.72, ...), channel_id=1, replica_groups=mesh['gx'=32,'vz_0'=4,'vz_1'=2] {'vz_0'}, use_global_device_ids=true, to_apply=%region_1.2 | all-reduce | flops 2560 | bytes 20480 | tf_op jit(solution)/shard_map/psum | solution.py:47
  202.5 9.0 %all-reduce.1 = (f32[8,64]{1,0:T(8,128)S(1)}, f32[8,64]{1,0:T(8,128)S(1)}, f32[8,64]{1,0:T(8,128)S(1)}, f32[8,64]{1,0:T(8,128)S(1)}, f32[8,64]{1,0:T(8,128)S(1)}) all-reduce(f32[8,64]{1,0:T(8,128)S(1)} %get-tuple-element.12, f32[8,64]{1,0:T(8,128)S(1)} %get-tuple-element.13, ...), channel_id=1, replica_groups=mesh['gx'=32,'vz_0'=4,'vz_1'=2] {'vz_1'}, use_global_device_ids=true, to_apply=%region_2.3 | all-reduce | flops 2560 | bytes 20480 | tf_op jit(solution)/shard_map/psum | solution.py:47
  211.5 0.1 copy.79
  211.8 0.1 copy.77
  212.0 0.2 multiply_add_fusion
  212.2 0.7 add_divide_fusion
  212.9 1.6 copy.81
  (36 shorter events, 1.3 us)
Async XLA Ops:
  3.5 14.6 %copy-start.3 = (s32[16]{0:T(128)S(1)}, s32[16]{0:T(128)}, u32[]{:S(2)}) copy-start(s32[16]{0:T(128)} %param.6) | copy-start | bytes 196
  3.5 56.2 %copy-start = (f32[16]{0:T(128)S(1)}, f32[16]{0:T(128)}, u32[]{:S(2)}) copy-start(f32[16]{0:T(128)} %param.7) | copy-start | bytes 196
  3.5 86.8 %all-to-all-start = ((f32[3,8,64,256]{3,1,0,2:T(8,128)}), f32[3,8,64,256]{3,1,0,2:T(8,128)S(1)}, u32[]{:S(2)}, u32[]{:S(2)}) async-start(f32[3,8,64,256]{3,1,0,2:T(8,128)} %copy.57), calls=%async_computation | async-start | bytes 3145728 | tf_op jit(solution)/shard_map/all_to_all | solution.py:15
  120.3 12.0 %copy-start.2 = (f32[8,64]{1,0:T(8,128)S(1)}, f32[8,64]{1,0:T(8,128)}, u32[]{:S(2)}) copy-start(f32[8,64]{1,0:T(8,128)} %param.8) | copy-start | bytes 6148
  120.3 12.3 %copy-start.1 = (f32[8,64]{1,0:T(8,128)S(1)}, f32[8,64]{1,0:T(8,128)}, u32[]{:S(2)}) copy-start(f32[8,64]{1,0:T(8,128)} %param.9) | copy-start | bytes 6148
  120.3 39.9 %all-to-all-start.1 = ((f32[3,256,2,256]{3,2,0,1:T(2,128)}), f32[3,256,2,256]{3,2,0,1:T(2,128)S(1)}, u32[]{:S(2)}, u32[]{:S(2)}) async-start(f32[3,256,2,256]{3,2,0,1:T(2,128)} %copy.61), calls=%async_computation.1 | async-start | bytes 3145728 | tf_op jit(solution)/shard_map/all_to_all | solution.py:85
  160.5 24.9 %collective-permute-start.1 = (f32[1,8,64,256]{3,1,2,0:T(8,128)S(1)}, f32[1,8,64,256]{3,1,2,0:T(8,128)S(1)}, u32[]{:S(2)}, u32[]{:S(2)}) collective-permute-start(f32[1,8,64,256]{3,1,2,0:T(8,128)S(1)} %bitcast.71), channel_id=1, source_target_pairs={{1,0},{2,1},{3,2},{4,3},{5,4},{6,5},{7,6},{9,8},{10,9},{11,10},{12... | collective-permute-start | bytes 1572872 | tf_op jit(solution)/shard_map/ppermute | solution.py:38
  178.1 9.7 %collective-permute-start = (f32[1,8,64,256]{3,1,2,0:T(8,128)}, f32[1,8,64,256]{3,1,2,0:T(8,128)S(1)}, u32[]{:S(2)}, u32[]{:S(2)}) collective-permute-start(f32[1,8,64,256]{3,1,2,0:T(8,128)} %bitcast.55), channel_id=1, source_target_pairs={{0,1},{1,2},{2,3},{3,4},{4,5},{5,6},{6,7},{8,9},{9,10},{10,11},{11... | collective-permute-start | bytes 1572872 | tf_op jit(solution)/shard_map/ppermute | solution.py:36
where the time goes:
time: 216 us; the launch traced here: 215 us
  between operations  70.4 us (33%)
  starting transfers between devices  46.3 us (21%)
  waiting for transfers between devices  33.7 us (16%)
  local copies, waits for them, and re-layouts  27.8 us (13%)
  blocking collectives  21.9 us (10%)
  other arithmetic  14.6 us (7%)
    all_to_all x1, waiting for transfers between devices, advect_columns(): lax.all_to_all(shifted, 'gx', split_axis=1, concat_axis=2, tiled=True)  27.6 us
    psum x2, blocking collectives, one_axis_at_a_time(): x = lax.psum(x, axis)  21.9 us
    ppermute x1, starting transfers between devices, padded_2(): lax.ppermute(head, axis, [((i + 1) % count, i) for i in range(ends)])  16.7 us
    concatenate x2, local copies, waits for them, and re-layouts, advect_columns(): doubled = jnp.concatenate([block, block], axis=1)  15.6 us
    all_to_all x1, starting transfers between devices, moved(): lax.all_to_all(group, axis, split_axis=split_dim, concat_axis=concat_dim,...  14.6 us
    all_to_all x1, starting transfers between devices, advect_columns(): lax.all_to_all(shifted, 'gx', split_axis=1, concat_axis=2, tiled=True)  11.8 us
    unnamed x15, other arithmetic  11.1 us
  transfers between devices with their start and end apart: 4, of which 3 were waited for; matrix products, arithmetic and copies ran while one was open for 2% of the time, Pallas kernels for 0%

commit v1 on v0

v1 whole, which is shorter than its diff:
```python
import functools
import math

import jax
import jax.numpy as jnp
from jax import lax
from jax.experimental import pallas as pl
from jax.experimental.pallas import tpu as pltpu
from jax.sharding import Mesh
from jax.sharding import PartitionSpec as P

AXES = ("x", "zh", "y", "zl", "core")
VZ = ("zl", "core")
GX = ("x", "zh", "y")
MESH = pl.DeviceIdType.MESH
HIGH = lax.Precision.HIGHEST

NVX = 16
COLS = 8
WIDE = 32
ROWS = 64
QUARTER = 16
PLANES = 3
TOTAL_VZ = 24
TR = 8
TILES = QUARTER // TR
CHUNKS = [(p, t) for p in (0, 2, 1) for t in range(TILES)]
N = len(CHUNKS)
FULL = 42

LANES = (slice(0, 128), slice(128, 256))
STEP_XY = 9.0 / 16
STEP_Z = 9.6 / TOTAL_VZ
CELL = STEP_XY * STEP_XY * STEP_Z


def kernel(
    cap,
    depth,
    sub,
    kick,
    rate,
    dens,
    out,
    *scratch,
):
    scratch = list(scratch)
    take = lambda k: [scratch.pop(0) for _ in range(k)]
    block, packed, lists, chosen, moved = (take(N) for _ in range(5))
    planes, kick_wide, plane_sums, part, parts, coef, wide, unit_col, unit_half, unit_turn = take(10)
    y1_own, y1_out, y1_in, z_out, z_in, x_out, x_in = take(7)
    y2_own, y2_out, y2_in, halo_out, halo_in, sum_out, sum_in = take(7)

    x, zh, y = (lax.axis_index(a) for a in GX)
    zl, core = (lax.axis_index(a) for a in VZ)
    nx = lax.axis_size("x")
    slab = zl * 2 + core
    slabs = lax.axis_size("zl") * 2

    def slab_device(v):
        return {"zl": v // 2, "core": v % 2}

    barrier = pltpu.get_barrier_semaphore()
    friends = [{"y": (y + k) % 4} for k in (1, 2, 3)]
    friends += [{"zh": 1 - zh}, {"x": (x + 1) % nx}, {"x": (x + nx - 1) % nx}]
    friends += [slab_device((slab + k) % slabs) for k in range(1, 8)]
    for friend in friends:
        pl.semaphore_signal(barrier, inc=1, device_id=friend, device_id_type=MESH)

    own = []
    for c, (p, t) in enumerate(CHUNKS):
        rows = pl.ds(y * QUARTER + t * TR, TR)
        own.append(
            [
                pltpu.make_async_copy(
                    dens.at[p, :, rows, LANES[h]], block[c].at[h, pl.ds(y * COLS, COLS)], y1_own.at[c, h]
                )
                for h in range(2)
            ]
        )
        for copy in own[c]:
            copy.start()
    pl.semaphore_wait(barrier, len(friends))

    def remote(src, dst, send, recv, device):
        return pltpu.make_async_remote_copy(
            src_ref=src, dst_ref=dst, send_sem=send, recv_sem=recv, device_id=device, device_id_type=MESH
        )

    y1 = []
    for c, (p, t) in enumerate(CHUNKS):
        group = []
        for k in range(3):
            to = (y + k + 1) % 4
            rows = pl.ds(to * QUARTER + t * TR, TR)
            for h in range(2):
                group.append(
                    remote(
                        dens.at[p, :, rows, LANES[h]],
                        block[c].at[h, pl.ds(y * COLS, COLS)],
                        y1_out.at[c, 2 * k + h],
                        y1_in.at[c, 2 * k + h],
                        {"y": to},
                    )
                )
                group[-1].start()
        y1.append(group)

    def next_unit(u, state):
        i, j = state
        d = depth[i]
        count = jnp.where(d >= 0, d + 1, -d)
        col = jnp.where(d >= 0, WIDE - 1 - d + j, j)
        unit_col[u] = jnp.minimum(jnp.maximum(col, 0), WIDE - 1)
        unit_half[u] = i >> 3
        unit_turn[u] = ((u - i) & 7) * 16
        last = j + 1 >= count
        return jnp.where(last, jnp.minimum(i + 1, NVX - 1), i), jnp.where(last, 0, j + 1)

    lax.fori_loop(0, cap * 8, next_unit, (jnp.int32(0), jnp.int32(0)))

    depths = [depth[i] for i in range(NVX)]
    first, start = [], jnp.int32(0)
    for d in depths:
        first.append(start + jnp.where(d >= 0, 1, -d - WIDE))
        start = start + jnp.where(d >= 0, d + 1, -d)
    side_rows = [jnp.where(d >= 0, 0, cap) for d in depths]

    lane_group = lax.broadcasted_iota(jnp.int32, (TR, 128), 1) >> 4

    def by_group(values, h):
        acc = jnp.full((TR, 128), values[h * 8])
        for s in range(1, 8):
            acc = jnp.where(lane_group == s, values[h * 8 + s], acc)
        return acc

    lane_depth = [by_group(depths, h) for h in range(2)]
    lane_far = [by_group([sub[i] for i in range(NVX)], h) for h in range(2)]

    pair = lax.broadcasted_iota(jnp.int32, (8, 256), 1)
    vx_of = ((pair >> 4).astype(jnp.float32) - 7.5) * STEP_XY
    vy_of = ((pair & 15).astype(jnp.float32) - 7.5) * STEP_XY
    which = lax.broadcasted_iota(jnp.int32, (8, 256), 0)
    weights = jnp.where(
        which == 0,
        1.0,
        jnp.where(which == 1, vx_of, jnp.where(which == 2, vy_of, jnp.where(which == 3, vx_of**2 + vy_of**2, 0.0))),
    )

    def spread(values, c):
        pick = (lax.broadcasted_iota(jnp.int32, (8, 128), 0) == c).astype(jnp.float32)
        return lax.dot_general(
            values, pick, (((0,), (0,)), ((), ())), precision=HIGH, preferred_element_type=jnp.float32
        )

    def widen_kick(c, _):
        kick_wide[c] = spread(kick[...], c)
        return 0

    lax.fori_loop(0, COLS, widen_kick, 0)

    @pl.when(slab == 0)
    def _():
        planes[0] = jnp.zeros((COLS, ROWS, 256), jnp.float32)

    @pl.when(slab == slabs - 1)
    def _():
        planes[4] = jnp.zeros((COLS, ROWS, 256), jnp.float32)

    z_copies, x_copies, y2, y2_self = {}, {}, {}, {}

    def stage_pack(c):
        for copy in own[c]:
            copy.wait()
        for copy in y1[c]:
            copy.wait_recv()

        def one_row(r, _):
            acc = None
            for s in range(8):
                u = r * 8 + s
                piece = pltpu.roll(block[c][unit_half[u], unit_col[u]], unit_turn[u], 1)
                acc = piece if s == 0 else jnp.where(lane_group == s, piece, acc)
            packed[c][r] = acc
            return 0

        lax.fori_loop(0, cap, one_row, 0)
        z_copies[c] = remote(
            packed[c], lists[c].at[pl.ds(zh * cap, cap)], z_out.at[c], z_in.at[c], {"zh": 1 - zh}
        )
        z_copies[c].start()

        def one_col(n, _):
            for h in range(2):
                acc = None
                for s in range(8):
                    col = jnp.minimum(jnp.maximum(n - 1 - depths[h * 8 + s], 0), WIDE - 1)
                    piece = block[c][h, col]
                    acc = piece if s == 0 else jnp.where(lane_group == s, piece, acc)
                chosen[c][n, :, h * 128 : h * 128 + 128] = acc
            return 0

        lax.fori_loop(0, WIDE + 1, one_col, 0)

    def stage_forward(c):
        z_copies[c].wait_recv()
        x_copies[c] = remote(
            lists[c].at[pl.ds((1 - zh) * cap, cap)],
            lists[c].at[pl.ds(zh * cap, cap)],
            x_out.at[c],
            x_in.at[c],
            {"x": (x + 1 - 2 * zh + nx) % nx},
        )
        x_copies[c].start()

    def stage_merge(c):
        x_copies[c].wait_recv()
        p, t = CHUNKS[c]

        def column(n):
            got = []
            for h in range(2):
                acc = None
                for s in range(8):
                    i = h * 8 + s
                    u = jnp.minimum(jnp.maximum(first[i] + n - 1, 0), cap * 8 - 1)
                    piece = pltpu.roll(lists[c][(u >> 3) + side_rows[i]], ((s - u) & 7) * 16, 1)
                    acc = piece if s == 0 else jnp.where(lane_group == s, piece, acc)
                from_col = n - 1 - lane_depth[h]
                local = jnp.logical_and(from_col >= 0, from_col < WIDE)
                got.append(jnp.where(local, chosen[c][n, :, h * 128 : h * 128 + 128], acc))
            return got

        def one_col(n, before):
            now = column(n)
            for h in range(2):
                moved[c][n - 1, :, h * 128 : h * 128 + 128] = (1.0 - lane_far[h]) * now[h] + lane_far[h] * before[h]
            return tuple(now)

        lax.fori_loop(1, WIDE + 1, one_col, tuple(column(0)))
        here = planes.at[p + 1, :, pl.ds(y * QUARTER + t * TR, TR), :]
        y2[c] = []
        for k in range(3):
            to = (y + k + 1) % 4
            y2[c].append(
                remote(moved[c].at[pl.ds(to * COLS, COLS)], here, y2_out.at[c, k], y2_in.at[c, k], {"y": to})
            )
            y2[c][k].start()
        y2_self[c] = pltpu.make_async_copy(moved[c].at[pl.ds(y * COLS, COLS)], here, y2_own.at[c])
        y2_self[c].start()

    down = remote(planes.at[1], planes.at[4], halo_out.at[0], halo_in.at[0], slab_device((slab + slabs - 1) % slabs))
    up = remote(planes.at[3], planes.at[0], halo_out.at[1], halo_in.at[1], slab_device((slab + 1) % slabs))

    def stage_plane(p):
        for c, (q, _) in enumerate(CHUNKS):
            if q == p:
                y2_self[c].wait()
                for k in range(3):
                    y2[c][k].wait_recv()
        if p == 0:
            pl.when(slab > 0)(down.start)
        if p == 2:
            pl.when(slab < slabs - 1)(up.start)

        def one_col(c, _):
            plane_sums[p, c] = lax.dot_general(
                weights,
                planes[p + 1, c],
                (((1,), (1,)), ((), ())),
                precision=HIGH,
                preferred_element_type=jnp.float32,
            )
            return 0

        lax.fori_loop(0, COLS, one_col, 0)

    for name, c in ORDER:
        {"A": stage_pack, "B": stage_forward, "C": stage_merge, "D": stage_plane}[name](c)

    a = kick[...]
    lift, drop, stay = jnp.maximum(a, 0.0), jnp.maximum(-a, 0.0), 1.0 - jnp.abs(a)
    totals = [jnp.zeros((COLS, ROWS), jnp.float32) for _ in range(5)]
    for p in range(PLANES):
        level = slab * PLANES + p
        up_on = jnp.where(level + 1 < TOTAL_VZ, lift, 0.0)
        down_on = jnp.where(level >= 1, drop, 0.0)
        vz = (level.astype(jnp.float32) - 11.5) * STEP_Z
        above = ((level + 1).astype(jnp.float32) - 11.5) * STEP_Z
        below = ((level - 1).astype(jnp.float32) - 11.5) * STEP_Z
        kept = stay + up_on + down_on
        lean = stay * vz + up_on * above + down_on * below
        heat = stay * (vz * vz) + up_on * (above * above) + down_on * (below * below)
        n0, n1, n2, n3 = (plane_sums[p, :, j, :] for j in range(4))
        for j, term in enumerate((n0 * kept, n1 * kept, n2 * kept, n0 * lean, n3 * kept + n0 * heat)):
            totals[j] = totals[j] + term
    for j in range(5):
        part[j, :, 0:ROWS] = totals[j]

    shares = []
    for k in range(7):
        shares.append(remote(part, parts.at[k], sum_out.at[k], sum_in.at[k], slab_device((slab + k + 1) % slabs)))
        shares[k].start()
    for k in range(7):
        shares[k].wait_recv()
    for j in range(5):
        for k in range(7):
            totals[j] = totals[j] + parts[k, j, :, 0:ROWS]

    mass = CELL * totals[0]
    flow_x = CELL * totals[1] / mass
    flow_y = CELL * totals[2] / mass
    flow_z = CELL * totals[3] / mass
    warm = (CELL * totals[4] - mass * (flow_x**2 + flow_y**2 + flow_z**2)) / (3.0 * mass)
    r = rate[...]
    share = 1.0 / (1.0 + r)
    two_pi_t = (2.0 * math.pi) * warm
    top = mass / (two_pi_t * jnp.sqrt(two_pi_t))
    for j, value in enumerate((share, r * share * top, -0.5 / warm, flow_x, flow_y, flow_z)):
        coef[j] = value

    pl.when(slab > 0)(up.wait_recv)
    pl.when(slab < slabs - 1)(down.wait_recv)

    def finish(c, _):
        for j in range(6):
            wide[j] = spread(coef[j], c)

        def rows_of(n, _):
            rows = pl.ds(pl.multiple_of(n * 8, 8), 8)
            keep, gain, cool, ux, uy, uz = (wide[j, rows, :] for j in range(6))
            a = kick_wide[c, rows, :]
            lift, drop, stay = jnp.maximum(a, 0.0), jnp.maximum(-a, 0.0), 1.0 - jnp.abs(a)
            for h in range(2):
                lanes = slice(h * 128, h * 128 + 128)
                flat = (vx_of[:, lanes] - ux) ** 2 + (vy_of[:, lanes] - uy) ** 2
                f = [planes[q, c, rows, lanes] for q in range(5)]
                for p in range(PLANES):
                    vz = ((slab * PLANES + p).astype(jnp.float32) - 11.5) * STEP_Z
                    bell = jnp.exp(cool * (flat + (vz - uz) ** 2))
                    kicked = stay * f[p + 1] + lift * f[p] + drop * f[p + 2]
                    out[p, c, rows, lanes] = keep * kicked + gain * bell
            return 0

        lax.fori_loop(0, ROWS // 8, rows_of, 0)
        return 0

    lax.fori_loop(0, COLS, finish, 0)

    pl.when(slab > 0)(down.wait_send)
    pl.when(slab < slabs - 1)(up.wait_send)
    for k in range(7):
        shares[k].wait_send()
    for c in range(N):
        z_copies[c].wait_send()
        x_copies[c].wait_send()
        for copy in y1[c] + y2[c]:
            copy.wait_send()


ORDER = (
    ("A", 0), ("A", 1), ("A", 2), ("B", 0), ("A", 3), ("C", 0), ("B", 1), ("A", 4), ("A", 5), ("C", 1), ("B", 2),
    ("C", 2), ("D", 0), ("B", 3), ("C", 3), ("B", 4), ("D", 2), ("C", 4), ("B", 5), ("C", 5), ("D", 1),
)


def step(cap, collective_id, density, shift_depth, sub_cell, gravity_kick, collision):
    f32 = jnp.float32
    vmem = pl.BlockSpec(memory_space=pltpu.VMEM)
    smem = pl.BlockSpec(memory_space=pltpu.SMEM)
    dma = pltpu.SemaphoreType.DMA
    return pl.pallas_call(
        functools.partial(kernel, cap),
        out_shape=jax.ShapeDtypeStruct((PLANES, COLS, ROWS, 256), f32),
        in_specs=[smem, smem, vmem, vmem, pl.BlockSpec(memory_space=pl.ANY)],
        out_specs=vmem,
        scratch_shapes=[pltpu.VMEM((2, WIDE, TR, 128), f32)] * N
        + [pltpu.VMEM((cap, TR, 128), f32)] * N
        + [pltpu.VMEM((2 * cap, TR, 128), f32)] * N
        + [pltpu.VMEM((WIDE + 1, TR, 256), f32)] * N
        + [pltpu.VMEM((WIDE, TR, 256), f32)] * N
        + [
            pltpu.VMEM((5, COLS, ROWS, 256), f32),
            pltpu.VMEM((COLS, ROWS, 128), f32),
            pltpu.VMEM((PLANES, COLS, 8, ROWS), f32),
            pltpu.VMEM((5, COLS, 128), f32),
            pltpu.VMEM((7, 5, COLS, 128), f32),
            pltpu.VMEM((6, COLS, ROWS), f32),
            pltpu.VMEM((6, ROWS, 128), f32),
            pltpu.SMEM((cap * 8,), jnp.int32),
            pltpu.SMEM((cap * 8,), jnp.int32),
            pltpu.SMEM((cap * 8,), jnp.int32),
            dma((N, 2)),
            dma((N, 6)),
            dma((N, 6)),
            dma((N,)),
            dma((N,)),
            dma((N,)),
            dma((N,)),
            dma((N,)),
            dma((N, 3)),
            dma((N, 3)),
            dma((2,)),
            dma((2,)),
            dma((7,)),
            dma((7,)),
        ],
        compiler_params=pltpu.CompilerParams(collective_id=collective_id, has_side_effects=True),
    )(shift_depth, sub_cell, gravity_kick, collision, density)


def per_device(density, shift_depth, sub_cell, gravity_kick, collision):
    return step(FULL, 1, density, shift_depth, sub_cell, gravity_kick, collision)


def solution(mesh):
    torus = Mesh(mesh.devices.reshape(mesh.shape["gx"] // 8, 2, 4, 4, 2), AXES)
    return jax.shard_map(
        per_device,
        mesh=torus,
        in_specs=(P(VZ, GX, None, None), P(), P(), P(GX, None), P(GX, None)),
        out_specs=P(VZ, GX, None, None),
        check_vma=False,
    )
```

time: 216 us -> 113 us (0.52)
  Pallas kernels: 0 us -> 110 us
  between operations: 70.4 us -> 0.01 us
  starting transfers between devices: 46.3 us -> 0 us
  waiting for transfers between devices: 33.7 us -> 0 us
  local copies, waits for them, and re-layouts: 27.8 us -> 2.7 us
  blocking collectives: 21.9 us -> 0 us
  other arithmetic: 14.6 us -> 0 us
    pallas_call x0 -> x1, Pallas kernels: none -> 110 us  [step(): pl.pallas_call(functools.partial(kernel, cap), out_shape=jax.ShapeDtypeSt...]
    all_to_all x2 -> x0, waiting for transfers between devices: 27.6 us -> none  [the longest x1 27.6 us: advect_columns(): lax.all_to_all(shifted, 'gx', split_axis=1, concat_axis=2, tiled=True)]
    all_to_all x2 -> x0, starting transfers between devices: 26.4 us -> none  [the longest x1 14.6 us: moved(): lax.all_to_all(group, axis, split_axis=split_dim, concat_axis=concat_dim,...]
    psum x2 -> x0, blocking collectives: 21.9 us -> none  [one_axis_at_a_time(): x = lax.psum(x, axis)]
    ppermute x2 -> x0, starting transfers between devices: 19.9 us -> none  [the longest x1 16.7 us: padded_2(): lax.ppermute(head, axis, [((i + 1) % count, i) for i in range(ends)])]
    concatenate x2 -> x0, local copies, waits for them, and re-layouts: 15.6 us -> none  [advect_columns(): doubled = jnp.concatenate([block, block], axis=1)]
    unnamed x15 -> x0, other arithmetic: 11.1 us -> none
    ppermute x2 -> x0, waiting for transfers between devices: 6.11 us -> none  [the longest x1 3.77 us: padded_2(): lax.ppermute(head, axis, [((i + 1) % count, i) for i in range(ends)])]
  transfers between devices with their start and end apart: 4 -> 0, of which waited for: 3 -> 0; matrix products, arithmetic and copies ran while one was open for 2% -> 0% of each run, Pallas kernels for 0% -> 0%
where the time goes in v1:
time: 113 us
  Pallas kernels  110 us (97%)
  local copies, waits for them, and re-layouts  2.7 us (2%)
    pallas_call x1, Pallas kernels, step(): pl.pallas_call(functools.partial(kernel, cap), out_shape=jax.ShapeDtypeSt...  110 us
    unnamed x1, local copies, waits for them, and re-layouts  2.7 us

profile of v1, /device:TPU:1, one launch (start us, length us, event | category | flops | bytes accessed | tf_op | source)
XLA Modules:
  0.0 112.8 jit_solution(2477229393620913775)
XLA Ops:
  0.0 110.1 %shard_map.55 = f32[3,8,64,256]{3,2,1,0:T(8,128)} custom-call(s32[16]{0:T(128)} %depth.1, f32[16]{0:T(128)} %sub.1, f32[8,64]{1,0:T(8,128)} %kick.1, f32[8,64]{1,0:T(8,128)} %rate.1, f32[3,8,64,256]{3,2,1,0:T(8,128)} %dens.1), custom_call_target="tpu_custom_call" | custom-call | tf_op jit(solution)/shard_map/pallas_call | solution.py:372
  110.1 2.7 %copy.7 = f32[3,8,64,256]{3,2,1,0:T(8,128)} copy(f32[3,8,64,256]{3,2,1,0:T(8,128)} %shard_map.55) | data formatting | bytes 3145728

commit v2 on v1

--- a/solution.py
+++ b/solution.py
@@ -27,6 +27,8 @@
 CHUNKS = [(p, t) for p in (0, 2, 1) for t in range(TILES)]
 N = len(CHUNKS)
 FULL = 42
+REACH = 21
+SPAN = WIDE + 2 * REACH
 
 LANES = (slice(0, 128), slice(128, 256))
 STEP_XY = 9.0 / 16
@@ -47,7 +49,7 @@
     scratch = list(scratch)
     take = lambda k: [scratch.pop(0) for _ in range(k)]
     block, packed, lists, chosen, moved = (take(N) for _ in range(5))
-    planes, kick_wide, plane_sums, part, parts, coef, wide, unit_col, unit_half, unit_turn = take(10)
+    planes, kick_wide, plane_sums, part, parts, coef, wide, order, local, remote_cols, mixed = take(11)
     y1_own, y1_out, y1_in, z_out, z_in, x_out, x_in = take(7)
     y2_own, y2_out, y2_in, halo_out, halo_in, sum_out, sum_in = take(7)
 
@@ -70,16 +72,8 @@
     own = []
     for c, (p, t) in enumerate(CHUNKS):
         rows = pl.ds(y * QUARTER + t * TR, TR)
-        own.append(
-            [
-                pltpu.make_async_copy(
-                    dens.at[p, :, rows, LANES[h]], block[c].at[h, pl.ds(y * COLS, COLS)], y1_own.at[c, h]
-                )
-                for h in range(2)
-            ]
-        )
-        for copy in own[c]:
-            copy.start()
+        own.append(pltpu.make_async_copy(dens.at[p, :, rows, :], block[c].at[pl.ds(y * COLS, COLS)], y1_own.at[c]))
+        own[c].start()
     pl.semaphore_wait(barrier, len(friends))
 
     def remote(src, dst, send, recv, device):
@@ -93,38 +87,59 @@
         for k in range(3):
             to = (y + k + 1) % 4
             rows = pl.ds(to * QUARTER + t * TR, TR)
-            for h in range(2):
-                group.append(
-                    remote(
-                        dens.at[p, :, rows, LANES[h]],
-                        block[c].at[h, pl.ds(y * COLS, COLS)],
-                        y1_out.at[c, 2 * k + h],
-                        y1_in.at[c, 2 * k + h],
-                        {"y": to},
-                    )
+            group.append(
+                remote(
+                    dens.at[p, :, rows, :],
+                    block[c].at[pl.ds(y * COLS, COLS)],
+                    y1_out.at[c, k],
+                    y1_in.at[c, k],
+                    {"y": to},
                 )
-                group[-1].start()
+            )
+            group[-1].start()
         y1.append(group)
 
-    def next_unit(u, state):
-        i, j = state
-        d = depth[i]
-        count = jnp.where(d >= 0, d + 1, -d)
-        col = jnp.where(d >= 0, WIDE - 1 - d + j, j)
-        unit_col[u] = jnp.minimum(jnp.maximum(col, 0), WIDE - 1)
-        unit_half[u] = i >> 3
-        unit_turn[u] = ((u - i) & 7) * 16
-        last = j + 1 >= count
-        return jnp.where(last, jnp.minimum(i + 1, NVX - 1), i), jnp.where(last, 0, j + 1)
-
-    lax.fori_loop(0, cap * 8, next_unit, (jnp.int32(0), jnp.int32(0)))
-
     depths = [depth[i] for i in range(NVX)]
-    first, start = [], jnp.int32(0)
-    for d in depths:
-        first.append(start + jnp.where(d >= 0, 1, -d - WIDE))
-        start = start + jnp.where(d >= 0, d + 1, -d)
-    side_rows = [jnp.where(d >= 0, 0, cap) for d in depths]
+    counts = [jnp.where(d >= 0, d + 1, -d) for d in depths]
+    ranks = [jnp.int32(0)] * NVX
+    for i in range(NVX):
+        for j in range(i):
+            behind = (counts[i] <= counts[j]).astype(jnp.int32)
+            ranks[i] = ranks[i] + behind
+            ranks[j] = ranks[j] + 1 - behind
+    places = [jnp.where(r < 8, r, 23 - r) for r in ranks]
+
+    def at_place(values, q):
+        acc = values[0]
+        for i in range(1, NVX):
+            acc = jnp.where(places[i] == q, values[i], acc)
+        return acc
+
+    depths = [at_place(depths, q) for q in range(NVX)]
+    far = [at_place([sub[i] for i in range(NVX)], q) for q in range(NVX)]
+    counts = [jnp.where(d >= 0, d + 1, -d) for d in depths]
+    edge = [REACH + jnp.where(d >= 0, WIDE - 1 - d, 0) for d in depths]
+    upper = edge[:8]
+    lower = [SPAN + edge[8 + s] - counts[s] for s in range(8)]
+    lists_at = [jnp.where(d >= 0, 0, cap - d - REACH) for d in depths]
+    for s in range(8):
+        lists_at[8 + s] = lists_at[8 + s] + counts[s]
+
+    to_lane = lax.broadcasted_iota(jnp.int32, (16, 256), 1)
+    to_sub = lax.broadcasted_iota(jnp.int32, (16, 256), 0)
+    for i in range(NVX):
+        order[i * 16 : i * 16 + 16, :] = (to_lane == places[i] * 16 + to_sub).astype(jnp.bfloat16)
+
+    def permute(values, back):
+        total = None
+        for _ in range(3):
+            piece = values.astype(jnp.bfloat16)
+            values = values - piece.astype(jnp.float32)
+            term = lax.dot_general(
+                piece, order[...], (((1,), (1 if back else 0,)), ((), ())), preferred_element_type=jnp.float32
+            )
+            total = term if total is None else total + term
+        return total
 
     lane_group = lax.broadcasted_iota(jnp.int32, (TR, 128), 1) >> 4
 
@@ -135,7 +150,7 @@
         return acc
 
     lane_depth = [by_group(depths, h) for h in range(2)]
-    lane_far = [by_group([sub[i] for i in range(NVX)], h) for h in range(2)]
+    lane_far = [by_group(far, h) for h in range(2)]
 
     pair = lax.broadcasted_iota(jnp.int32, (8, 256), 1)
     vx_of = ((pair >> 4).astype(jnp.float32) - 7.5) * STEP_XY
@@ -170,16 +185,21 @@
     z_copies, x_copies, y2, y2_self = {}, {}, {}, {}
 
     def stage_pack(c):
-        for copy in own[c]:
-            copy.wait()
+        own[c].wait()
         for copy in y1[c]:
             copy.wait_recv()
+
+        for b in range(2):
+            cols = slice(b * 16, b * 16 + 16)
+            lined = permute(block[c][cols].reshape(16 * TR, 256), False)
+            for h in range(2):
+                at = h * SPAN + REACH + b * 16
+                local[at : at + 16] = lined[:, LANES[h]].reshape(16, TR, 128)
 
         def one_row(r, _):
             acc = None
             for s in range(8):
-                u = r * 8 + s
-                piece = pltpu.roll(block[c][unit_half[u], unit_col[u]], unit_turn[u], 1)
+                piece = local[r + jnp.where(r < counts[s], upper[s], lower[s])]
                 acc = piece if s == 0 else jnp.where(lane_group == s, piece, acc)
             packed[c][r] = acc
             return 0
@@ -194,10 +214,9 @@
             for h in range(2):
                 acc = None
                 for s in range(8):
-                    col = jnp.minimum(jnp.maximum(n - 1 - depths[h * 8 + s], 0), WIDE - 1)
-                    piece = block[c][h, col]
+                    piece = local[n + (h * SPAN + REACH - 1 - depths[h * 8 + s])]
                     acc = piece if s == 0 else jnp.where(lane_group == s, piece, acc)
-                chosen[c][n, :, h * 128 : h * 128 + 128] = acc
+                chosen[c][n, :, LANES[h]] = acc
             return 0
 
         lax.fori_loop(0, WIDE + 1, one_col, 0)
@@ -217,27 +236,38 @@
         x_copies[c].wait_recv()
         p, t = CHUNKS[c]
 
+        def one_remote(j, _):
+            for h in range(2):
+                acc = None
+                for s in range(8):
+                    piece = lists[c][j + lists_at[h * 8 + s]]
+                    acc = piece if s == 0 else jnp.where(lane_group == s, piece, acc)
+                remote_cols[j + 12, :, LANES[h]] = acc
+            return 0
+
+        lax.fori_loop(0, REACH, one_remote, 0)
+
         def column(n):
             got = []
             for h in range(2):
-                acc = None
-                for s in range(8):
-                    i = h * 8 + s
-                    u = jnp.minimum(jnp.maximum(first[i] + n - 1, 0), cap * 8 - 1)
-                    piece = pltpu.roll(lists[c][(u >> 3) + side_rows[i]], ((s - u) & 7) * 16, 1)
-                    acc = piece if s == 0 else jnp.where(lane_group == s, piece, acc)
                 from_col = n - 1 - lane_depth[h]
-                local = jnp.logical_and(from_col >= 0, from_col < WIDE)
-                got.append(jnp.where(local, chosen[c][n, :, h * 128 : h * 128 + 128], acc))
+                inside = jnp.logical_and(from_col >= 0, from_col < WIDE)
+                beyond = jnp.where(
+                    lane_depth[h] >= 0, remote_cols[n + 12, :, LANES[h]], remote_cols[n, :, LANES[h]]
+                )
+                got.append(jnp.where(inside, chosen[c][n, :, LANES[h]], beyond))
             return got
 
         def one_col(n, before):
             now = column(n)
             for h in range(2):
-                moved[c][n - 1, :, h * 128 : h * 128 + 128] = (1.0 - lane_far[h]) * now[h] + lane_far[h] * before[h]
+                mixed[n - 1, :, LANES[h]] = (1.0 - lane_far[h]) * now[h] + lane_far[h] * before[h]
             return tuple(now)
 
         lax.fori_loop(1, WIDE + 1, one_col, tuple(column(0)))
+        for b in range(2):
+            cols = slice(b * 16, b * 16 + 16)
+            moved[c][cols] = permute(mixed[cols].reshape(16 * TR, 256), True).reshape(16, TR, 256)
         here = planes.at[p + 1, :, pl.ds(y * QUARTER + t * TR, TR), :]
         y2[c] = []
         for k in range(3):
@@ -374,9 +404,9 @@
         out_shape=jax.ShapeDtypeStruct((PLANES, COLS, ROWS, 256), f32),
         in_specs=[smem, smem, vmem, vmem, pl.BlockSpec(memory_space=pl.ANY)],
         out_specs=vmem,
-        scratch_shapes=[pltpu.VMEM((2, WIDE, TR, 128), f32)] * N
+        scratch_shapes=[pltpu.VMEM((WIDE, TR, 256), f32)] * N
         + [pltpu.VMEM((cap, TR, 128), f32)] * N
-        + [pltpu.VMEM((2 * cap, TR, 128), f32)] * N
+        + [pltpu.VMEM((max(2 * cap, cap + 2 * REACH), TR, 128), f32)] * N
         + [pltpu.VMEM((WIDE + 1, TR, 256), f32)] * N
         + [pltpu.VMEM((WIDE, TR, 256), f32)] * N
         + [
@@ -387,12 +417,13 @@
             pltpu.VMEM((7, 5, COLS, 128), f32),
             pltpu.VMEM((6, COLS, ROWS), f32),
             pltpu.VMEM((6, ROWS, 128), f32),
-            pltpu.SMEM((cap * 8,), jnp.int32),
-            pltpu.SMEM((cap * 8,), jnp.int32),
-            pltpu.SMEM((cap * 8,), jnp.int32),
-            dma((N, 2)),
-            dma((N, 6)),
-            dma((N, 6)),
+            pltpu.VMEM((256, 256), jnp.bfloat16),
+            pltpu.VMEM((2 * SPAN + 2 * REACH, TR, 128), f32),
+            pltpu.VMEM((REACH + 24, TR, 256), f32),
+            pltpu.VMEM((WIDE, TR, 256), f32),
+            dma((N,)),
+            dma((N, 3)),
+            dma((N, 3)),
             dma((N,)),
             dma((N,)),
             dma((N,)),

time: 113 us -> 100 us (0.88)
  Pallas kernels: 110 us -> 97.6 us
    pallas_call x1, Pallas kernels: 110 us -> 97.6 us  [step(): pl.pallas_call(functools.partial(kernel, cap), out_shape=jax.ShapeDtypeSt...]
where the time goes in v2:
time: 100 us
  Pallas kernels  97.6 us (98%)
  local copies, waits for them, and re-layouts  2.7 us (3%)
    pallas_call x1, Pallas kernels, step(): pl.pallas_call(functools.partial(kernel, cap), out_shape=jax.ShapeDtypeSt...  97.6 us
    unnamed x1, local copies, waits for them, and re-layouts  2.7 us

profile of v2, /device:TPU:1, one launch (start us, length us, event | category | flops | bytes accessed | tf_op | source)
XLA Modules:
  0.0 100.3 jit_solution(691347894394999172)
XLA Ops:
  0.0 97.6 %shard_map.55 = f32[3,8,64,256]{3,2,1,0:T(8,128)} custom-call(s32[16]{0:T(128)} %depth.1, f32[16]{0:T(128)} %sub.1, f32[8,64]{1,0:T(8,128)} %kick.1, f32[8,64]{1,0:T(8,128)} %rate.1, f32[3,8,64,256]{3,2,1,0:T(8,128)} %dens.1), custom_call_target="tpu_custom_call" | custom-call | tf_op jit(solution)/shard_map/pallas_call | solution.py:402
  97.6 2.7 %copy.7 = f32[3,8,64,256]{3,2,1,0:T(8,128)} copy(f32[3,8,64,256]{3,2,1,0:T(8,128)} %shard_map.55) | data formatting | bytes 3145728
